TPU v7x, 128 devices: a whole 4x4x4 slice. The times are simulated.
128 devices in a mesh: row: 8 (over x, core), col: 16 (over y, z).
Axes of the slice: x: 4, y: 4, z: 4, core: 2. Of those that a mesh axis runs over, the one named last changes fastest.
Arguments:
- filtered: float32 [32768, 2048], P(('row', 'col')), as said below
- hamiltonian_applied: float32 [32768, 2048], P(('row', 'col')), as said below
- rotation: float32 [2048, 2048], replicated, may hold values from -0.125 to 0.125
Outputs:
- intersection: float32 [2048, 2048], P('row', 'col')
- projected: float32 [2048, 2048], P('row', 'col')
- rotated: float32 [32768, 2048], P(('row', 'col'))
Inputs may be any that keep to these rules, and one draw needn't show every extreme that they name: `filtered`: finite real values. `hamiltonian_applied`: finite real values.
All inputs are finite; a program needn't handle non-finite values.
Results may differ from a plain program's by a relative error of at most 0.00005.
Values sent between devices are 32-bit elements; how exact they have to be, the bound alone decides.
A program may use at most 192 MiB of HBM per device.

v0:
```python
import jax
import jax.numpy as jnp
from jax import lax
from jax.sharding import PartitionSpec as P


def inner_rows(first, second):
    return jnp.einsum(
        "gi,gj->ij",
        first,
        second,
        precision=lax.Precision.HIGHEST,
        preferred_element_type=jnp.float32,
    )


def product(first, second):
    return jnp.dot(
        first, second, precision=lax.Precision.HIGHEST, preferred_element_type=jnp.float32
    )


def local(filtered, hamiltonian_applied, rotation):
    cells = filtered.shape[0]
    col_count = lax.axis_size("col")
    row_count = lax.axis_size("row")
    scale = 1.0 / (cells * col_count * row_count)
    psi_band, ham_band = (
        lax.all_to_all(filtered, "col", split_axis=1, concat_axis=0, tiled=True),
        lax.all_to_all(hamiltonian_applied, "col", split_axis=1, concat_axis=0, tiled=True),
    )
    piece = lax.all_gather(psi_band, "col", axis=1, tiled=True)
    over_term = inner_rows(piece, psi_band) * scale
    proj_term = inner_rows(piece, ham_band) * scale
    over_term, proj_term = (over_term, proj_term)
    intersection, projected = (
        lax.psum_scatter(over_term, "row", scatter_dimension=0, tiled=True),
        lax.psum_scatter(proj_term, "row", scatter_dimension=0, tiled=True),
    )
    rotated = product(filtered, rotation)
    return (intersection, projected, rotated)


def solution(mesh):
    return jax.shard_map(
        local,
        mesh=mesh,
        in_specs=(P(("row", "col"), None), P(("row", "col"), None), P()),
        out_specs=(P("row", "col"), P("row", "col"), P(("row", "col"), None)),
        check_vma=False,
    )
```

profile of v0, /device:TPU:1, one launch (start us, length us, event | category | flops | bytes accessed | tf_op | source)
XLA Modules:
  0.0 424.3 jit_solution(1615125823483766629)
XLA Ops:
  7.2 0.0 all-gather.2.cloned.1.call-start
  7.2 2.9 copy.6
  10.1 35.1 %all_to_all.38 = f32[256,16,128]{0,2,1:T(8,128)S(1)} all-to-all(f32[256,16,128]{0,2,1:T(8,128)} %bitcast.17), channel_id=1, replica_groups=mesh['row'=8,'col'=16] {'col'}, dimensions={1} | all-to-all | bytes 4194304 | tf_op jit(solution)/shard_map/all_to_all | solution.py:29
  45.2 1.8 copy.7
  47.0 0.0 copy-start.2
  47.0 0.0 all-gather.2.cloned.1.call-update
  47.0 1.6 copy-done.2
  48.6 1.9 copy.8
  50.5 0.0 copy-start
  50.5 4.6 %all-to-all-start.1 = ((f32[256,16,128]{0,2,1:T(8,128)}), f32[256,16,128]{0,2,1:T(8,128)}, u32[]{:S(2)}, u32[]{:S(2)}) async-start(f32[256,16,128]{0,2,1:T(8,128)} %bitcast.15), calls=%async_computation.2 | async-start | bytes 4194304 | tf_op jit(solution)/shard_map/all_to_all | solution.py:30
  55.1 0.0 reduce-scatter.3.cloned.1.call-start
  55.2 216.2 %all-gather.2.cloned.1.call-done = f32[4096,2048]{1,0:T(8,128)} async-done(((f32[4096,128]{1,0:T(8,128)}), f32[4096,2048]{1,0:T(8,128)}) %all-gather.2.cloned.1.call-update) | async-done | bytes 33554448 | tf_op jit(solution)/shard_map/all_gather | solution.py:32
  271.4 0.0 copy-done
  271.4 56.6 %convolution_multiply_fusion.1 = f32[2048,128]{1,0:T(8,128)} fusion(f32[4096,2048]{1,0:T(8,128)} %all-gather.2.cloned.1.call-done, f32[4096,128]{1,0:T(8,128)S(1)} %bitcast.13), kind=kOutput, calls=%fused_computation.1 | convolution fusion | flops 12885164032 | bytes 36700160 | tf_op jit(solution)/shard_map/gi,gj->ij/dot_general | solution.py:8
  328.0 0.0 reduce-scatter.3.cloned.1.call-update
  328.0 0.0 reduce-scatter.5.cloned.1.call-start
  328.1 0.0 all-to-all-done.1
  328.1 2.9 copy.9
  331.0 0.0 copy-start.1
  331.0 57.4 %convolution_multiply_fusion = f32[2048,128]{1,0:T(8,128)} fusion(f32[4096,2048]{1,0:T(8,128)} %all-gather.2.cloned.1.call-done, f32[4096,128]{1,0:T(8,128)} %bitcast.14), kind=kOutput, calls=%fused_computation | convolution fusion | flops 12885164032 | bytes 36700160 | tf_op jit(solution)/shard_map/gi,gj->ij/dot_general | solution.py:8
  388.4 0.0 reduce-scatter.5.cloned.1.call-update
  388.4 0.0 copy-done.1
  388.4 17.8 %fusion = f32[256,2048]{1,0:T(8,128)} fusion(f32[256,2048]{1,0:T(8,128)S(1)} %copy-done.1, f32[2048,2048]{1,0:T(8,128)} %param.5), kind=kOutput, calls=%fused_computation.2 | convolution fusion | flops 12884901888 | bytes 20971520 | tf_op jit(solution)/shard_map/dot_general | solution.py:18
  406.2 0.0 reduce-scatter.3.cloned.1.call-done
  406.2 11.5 %reduce-scatter.5.cloned.1.call-done = f32[256,128]{1,0:T(8,128)} async-done(((f32[2048,128]{1,0:T(8,128)}), f32[256,128]{1,0:T(8,128)}) %reduce-scatter.5.cloned.1.call-update) | async-done | bytes 131088 | tf_op jit(solution)/shard_map/reduce_scatter | solution.py:38
Async XLA Ops:
  7.2 264.2 %all-gather.2.cloned.1.call-start = ((), (), s32[]{:S(2)}) async-start(), calls=%async_computation.4 | async-start | bytes 35651584 | tf_op jit(solution)/shard_map/all_gather | solution.py:32
  47.0 1.6 copy-start.2
  50.5 220.9 %copy-start = (f32[16,256,128]{2,1,0:T(8,128)S(1)}, f32[16,256,128]{2,1,0:T(8,128)}, u32[]{:S(2)}) copy-start(f32[16,256,128]{2,1,0:T(8,128)} %copy.7) | copy-start | bytes 6291460
  50.5 277.6 %all-to-all-start.1 = ((f32[256,16,128]{0,2,1:T(8,128)}), f32[256,16,128]{0,2,1:T(8,128)}, u32[]{:S(2)}, u32[]{:S(2)}) async-start(f32[256,16,128]{0,2,1:T(8,128)} %bitcast.15), calls=%async_computation.2 | async-start | bytes 4194304 | tf_op jit(solution)/shard_map/all_to_all | solution.py:30
  55.1 351.1 %reduce-scatter.3.cloned.1.call-start = ((), (), s32[]{:S(2)}) async-start(), calls=%async_computation.5 | async-start | bytes 1179648 | tf_op jit(solution)/shard_map/reduce_scatter | solution.py:37
  328.0 89.7 %reduce-scatter.5.cloned.1.call-start = ((), (), s32[]{:S(2)}) async-start(), calls=%async_computation.6 | async-start | bytes 1179648 | tf_op jit(solution)/shard_map/reduce_scatter | solution.py:38
  331.0 57.4 %copy-start.1 = (f32[256,2048]{1,0:T(8,128)S(1)}, f32[256,2048]{1,0:T(8,128)}, u32[]{:S(2)}) copy-start(f32[256,2048]{1,0:T(8,128)} %param.3) | copy-start | bytes 6291460
Sparse Core Ops, SparseCore 0:
  47.1 224.1 all-gather.1
  328.1 29.1 reduce-scatter.2
  388.5 29.1 reduce-scatter.4
where the time goes:
time: 427 us; the launch traced here: 424 us
  waiting for transfers between devices  228 us (53%)
  matrix products  132 us (31%)
  blocking collectives  35.1 us (8%)
  between operations  13.8 us (3%)
  local copies, waits for them, and re-layouts  11 us (3%)
  starting transfers between devices  4.76 us (1%)
    all_gather x1, waiting for transfers between devices, local(): piece = lax.all_gather(psi_band, 'col', axis=1, tiled=True)  216 us
    dot_general x2, matrix products, inner_rows(): jnp.einsum('gi,gj->ij', first, second, precision=lax.Precision.HIGHEST, p...  114 us
    all_to_all x1, blocking collectives, local(): lax.all_to_all(filtered, 'col', split_axis=1, concat_axis=0, tiled=True)  35.1 us
    dot_general x1, matrix products, product(): jnp.dot(first, second, precision=lax.Precision.HIGHEST, preferred_element...  17.8 us
    reduce_scatter x1, waiting for transfers between devices, local(): lax.psum_scatter(proj_term, 'row', scatter_dimension=0, tiled=True)  11.5 us
  transfers between devices with their start and end apart: 4, of which 2 were waited for; matrix products, arithmetic and copies ran while one was open for 32% of the time, Pallas kernels for 0%

commit v1 on v0

v1 whole, which is shorter than its diff:
```python
import jax
import jax.numpy as jnp
from jax import lax
from jax.experimental import pallas as pl
from jax.experimental.pallas import tpu as pltpu
from jax.sharding import PartitionSpec as P

MESH = pl.DeviceIdType.MESH
F32 = jnp.float32
BF16 = jnp.bfloat16
ROWS = 256
M = 2048
TILE = 128
BAND = 144
EARLY = 2
CHUNK = 256


def split(value):
    high = value.astype(BF16)
    low = (value - high.astype(F32)).astype(BF16)
    return high, low


def dot(first, second):
    return jnp.dot(first, second, preferred_element_type=F32)


def dot3(first_high, first_low, second_high, second_low):
    return dot(first_high, second_high) + dot(first_high, second_low) + dot(first_low, second_high)


class Ring:
    def __init__(self, block, landing, send, recv, me, right, left):
        def copy(m):
            source, device = self.routes[m]
            return pltpu.make_async_remote_copy(
                src_ref=source,
                dst_ref=landing(m),
                send_sem=send(m),
                recv_sem=recv(m),
                device_id=device,
                device_id_type=MESH,
            )

        opposite, after, before = (lax.rem(me + n, 4) for n in (2, 1, 3))
        self.after, self.before = block(after, 0), block(before, 1)
        self.landing = landing
        self.mine = (block(me, 0), block(me, 1))
        self.copy = copy
        self.routes = (
            (block(opposite, 0), right),
            (block(opposite, 1), left),
            (block(after, 1), right),
            (block(before, 0), left),
            (self.after, right),
            (self.before, left),
        )

    def start(self, *messages):
        for m in messages:
            self.copy(m).start()

    def forward(self):
        self.copy(0).wait_recv()
        self.after[...] = self.after[...] + self.landing(0)[...]
        self.copy(4).start()
        self.copy(1).wait_recv()
        self.before[...] = self.before[...] + self.landing(1)[...]
        self.copy(5).start()

    def total(self, half):
        left, right = ((4, 3), (2, 5))[half]
        self.copy(left).wait_recv()
        self.copy(right).wait_recv()
        return self.mine[half][...] + self.landing(left)[...] + self.landing(right)[...]

    def drain(self):
        for m in range(6):
            self.copy(m).wait_send()


def kernel(
    psi_hbm, ham_hbm, rot_hbm, over_ref, proj_ref, rotated_hbm,
    raw_a, raw_b, pair_a, pair_b, ah, al, bh, bl, ath, atl,
    rot_buf, out_buf,
    da, db, dc, xa1, xb1, xc1, ea, eb, ec, xa2, xb2, xc2, fa, fb, fc, xa3, xb3, xc3, piece, final,
    sa1, ra1, sb1, rb1, sc1, rc1, s2, r2, s3, r3, s_pair, r_pair, s_fin, r_fin, load_sem, rot_sem, out_sem,
):
    row, col = lax.axis_index("row"), lax.axis_index("col")
    x, core = row // 2, lax.rem(row, 2)
    y, z = col // 4, lax.rem(col, 4)

    def chip(dx=0, dy=0, dz=0):
        return (
            2 * lax.rem(x + dx, 4) + core,
            4 * lax.rem(y + dy, 4) + lax.rem(z + dz, 4),
        )

    partner = (2 * x + 1 - core, col)
    x_right, x_left = chip(dx=1), chip(dx=3)
    y_right, y_left = chip(dy=1), chip(dy=3)
    z_right, z_left = chip(dz=1), chip(dz=3)

    barrier = pltpu.get_barrier_semaphore()
    for device in (partner, x_right, x_left, y_right, y_left, z_right, z_left):
        pl.semaphore_signal(barrier, inc=1, device_id=device, device_id_type=MESH)

    load_a = pltpu.make_async_copy(psi_hbm, raw_a, load_sem.at[0])
    load_b = pltpu.make_async_copy(ham_hbm, raw_b, load_sem.at[1])
    load_a.start()
    load_b.start()

    def rot_load(n):
        slot = lax.rem(n, 2)
        columns = pl.ds(pl.multiple_of(n * CHUNK, CHUNK), CHUNK)
        return pltpu.make_async_copy(rot_hbm.at[:, columns], rot_buf.at[slot], rot_sem.at[slot])

    def rotated_store(n):
        slot = lax.rem(n, 2)
        columns = pl.ds(pl.multiple_of(n * CHUNK, CHUNK), CHUNK)
        return pltpu.make_async_copy(out_buf.at[slot], rotated_hbm.at[:, columns], out_sem.at[slot])

    rot_load(0).start()
    rot_load(1).start()
    pl.semaphore_wait(barrier, 7)

    def pair_copy(source, target, n):
        return pltpu.make_async_remote_copy(
            src_ref=source,
            dst_ref=target,
            send_sem=s_pair.at[n],
            recv_sem=r_pair.at[n],
            device_id=partner,
            device_id_type=MESH,
        )

    pairs = [pair_copy(psi_hbm, pair_a, 0), pair_copy(ham_hbm, pair_b, 1)]
    for copy in pairs:
        copy.start()

    def prepare(raw, high, low, base):
        @pl.loop(0, 8)
        def _(j):
            columns = pl.ds(pl.multiple_of(j * 256, 256), 256)
            h, l = split(raw[:, columns])
            high[base : base + ROWS, columns] = h
            low[base : base + ROWS, columns] = l

    def turn(raw, base):
        @pl.loop(0, 4)
        def _(block):
            start = (2 * block + core) * 256
            h, l = split(raw[:, pl.ds(pl.multiple_of(start, 256), 256)].T)
            ath[block, :, base : base + ROWS] = h
            atl[block, :, base : base + ROWS] = l

    load_a.wait()
    prepare(raw_a, ah, al, 0)
    turn(raw_a, 0)
    load_b.wait()
    prepare(raw_b, bh, bl, 0)

    def rotated_chunk(n):
        slot = lax.rem(n, 2)
        rot_load(n).wait()
        acc = jnp.zeros((ROWS, CHUNK), F32)
        for k in range(8):
            h, l = split(rot_buf[slot, 256 * k : 256 * k + 256, :])
            cut = slice(256 * k, 256 * k + 256)
            acc = acc + dot3(ah[0:ROWS, cut], al[0:ROWS, cut], h, l)

        @pl.when(n >= 2)
        def _():
            rotated_store(n - 2).wait()

        out_buf[slot] = acc
        rotated_store(n).start()

        @pl.when(n + 2 < M // CHUNK)
        def _():
            rot_load(n + 2).start()

    pl.loop(0, EARLY)(rotated_chunk)

    pairs[0].wait_recv()
    prepare(pair_a, ah, al, ROWS)
    turn(pair_a, ROWS)
    pairs[1].wait_recv()
    prepare(pair_b, bh, bl, ROWS)

    y_off = ((2, 1), (3, 0))

    def ring_a1(s):
        return Ring(
            lambda u, h: da.at[u, lax.rem(y + y_off[s][h], 4)],
            lambda m: xa1.at[s, m],
            lambda m: sa1.at[s, m],
            lambda m: ra1.at[s, m],
            x, x_right, x_left,
        )

    def block_of(step):
        return lax.rem(x + 2 + 3 * step + 3 * (step // 2) + 2 * (step // 3), 4)

    def ring_b1(step):
        block = block_of(step)
        return Ring(
            lambda u, h: db.at[block, u, 2 * h : 2 * h + 2],
            lambda m: xb1.at[step, m],
            lambda m: sb1.at[step, m],
            lambda m: rb1.at[step, m],
            y, y_right, y_left,
        )

    def ring_c1(step):
        block = block_of(step)
        return Ring(
            lambda u, h: dc.at[block, u, 2 * h : 2 * h + 2],
            lambda m: xc1.at[step, m],
            lambda m: sc1.at[step, m],
            lambda m: rc1.at[step, m],
            z, z_right, z_left,
        )

    a_rings = [ring_a1(0), ring_a1(1)]

    @pl.loop(0, 4)
    def _(step):
        block = block_of(step)
        strip = 2 * block + core
        b_ring, c_ring = ring_b1(step), ring_c1(step)
        for i, off in enumerate((2, 1, 3, 0)):
            yy = lax.rem(y + off, 4)
            columns = pl.ds(pl.multiple_of(yy * 512, 512), 512)
            acc = dot3(ath[block], atl[block], bh[:, columns], bl[:, columns])
            for t in range(4):
                da[block, yy, t] = acc[0:TILE, TILE * t : TILE * t + TILE]
                db[block, yy, t] = acc[TILE:ROWS, TILE * t : TILE * t + TILE]
            s, h = i // 2, i % 2

            @pl.when(step == 0)
            def _():
                a_rings[s].start(h)

            if h == 1:

                @pl.when(step == 1)
                def _():
                    a_rings[s].start(2)
            else:

                @pl.when(step == 2)
                def _():
                    a_rings[s].start(3)

            if i == 0:
                b_ring.start(0, 1)
            elif i == 1:
                b_ring.start(2)
            elif i == 2:
                b_ring.start(3)
            if i == 0:
                for j in range(5):
                    start = lax.rem(strip + j, 8) * 256
                    columns = pl.ds(pl.multiple_of(start, 256), 256)
                    acc = dot3(ath[block], atl[block], ah[:, columns], al[:, columns])
                    if j < 4:
                        tiles = [(2 * j, acc[:, 0:TILE]), (2 * j + 1, acc[:, TILE:256])]
                    else:
                        swap = strip >= 4
                        top = jnp.where(swap, acc[0:TILE, TILE:256], acc[0:TILE, 0:TILE])
                        low = jnp.where(swap, acc[TILE:ROWS, 0:TILE], acc[TILE:ROWS, TILE:256])
                        tiles = [(8, jnp.concatenate([top, low], axis=0))]
                    for t, tile in tiles:
                        dc[block, :, :, 16 * t : 16 * t + 16, :] = tile.reshape(4, 4, 16, TILE)
                c_ring.start(0, 1, 2, 3)

        @pl.when(step >= 1)
        def _():
            ring_c1(step - 1).forward()
            ring_b1(step - 1).forward()

    ring_c1(3).forward()
    ring_b1(3).forward()
    for ring in a_rings:
        ring.forward()

    pl.loop(EARLY, M // CHUNK)(rotated_chunk)

    def ring_n(stage, part, block, landing, me, right, left):
        send, recv = (s2, r2) if stage == 2 else (s3, r3)
        return Ring(
            block, lambda m: landing.at[m], lambda m: send.at[part, m], lambda m: recv.at[part, m],
            me, right, left,
        )

    ring_a2 = ring_n(2, 0, lambda u, h: ea.at[u, 2 * h : 2 * h + 2], xa2, y, y_right, y_left)
    ring_b2 = ring_n(2, 1, lambda u, h: eb.at[u, 2 * h : 2 * h + 2], xb2, z, z_right, z_left)
    ring_c2 = ring_n(2, 2, lambda u, h: ec.at[u, 2 * h : 2 * h + 2], xc2, x, x_right, x_left)

    @pl.loop(0, 4)
    def _(step):
        ring = ring_c1(step)
        for h in range(2):
            ec[block_of(step), 2 * h : 2 * h + 2] = ring.total(h)

    ring_c2.start(0, 1, 2, 3)
    for s in range(2):
        for h in range(2):
            ea[lax.rem(y + y_off[s][h], 4)] = a_rings[s].total(h)
    ring_a2.start(0, 1, 2, 3)

    @pl.loop(0, 4)
    def _(step):
        ring = ring_b1(step)
        for h in range(2):
            eb[2 * h : 2 * h + 2, block_of(step)] = ring.total(h)

    ring_b2.start(0, 1, 2, 3)
    for ring in (ring_c2, ring_a2, ring_b2):
        ring.forward()

    half = lambda ref, n: lambda u, h: ref.at[u, n * h : n * h + n]
    ring_a3 = ring_n(3, 0, half(fa, 64), xa3, z, z_right, z_left)
    ring_b3 = ring_n(3, 1, half(fb, 64), xb3, x, x_right, x_left)
    ring_c3 = ring_n(3, 2, half(fc, 72), xc3, y, y_right, y_left)
    for ring, ref, nxt in ((ring_c2, fc, ring_c3), (ring_a2, fa, ring_a3), (ring_b2, fb, ring_b3)):
        for h in range(2):
            ref[2 * h : 2 * h + 2] = ring.total(h)
        nxt.start(0, 1, 2, 3)
    for ring in (ring_c3, ring_a3, ring_b3):
        ring.forward()

    for h in range(2):
        piece[72 * h : 72 * h + 72] = ring_c3.total(h)
    scale = 1.0 / (ROWS * 128)
    strip = row
    part = 4 * z + y
    part_half, part_rest = part // 8, lax.rem(part, 8)
    slot = pl.ds(pl.multiple_of(16 * part_rest, 16), 16)
    remote, local = [], []
    for t in range(9):
        other = lax.rem(strip + t // 2, 8)
        side = t % 2 if t < 8 else lax.rem(part_half + strip // 4, 2)
        source = piece.at[16 * t : 16 * t + 16]
        target = 2 * other + side

        def fin(n, device, place):
            return pltpu.make_async_remote_copy(
                src_ref=source,
                dst_ref=place,
                send_sem=s_fin.at[n],
                recv_sem=r_fin.at[0],
                device_id=device,
                device_id_type=MESH,
            )

        direct = fin(t, (strip, target), final.at[part_half, slot])
        stay = pltpu.make_async_copy(source, final.at[part_half, slot], r_fin.at[0])
        pl.when(target != col)(direct.start)
        pl.when(target == col)(stay.start)
        local.append((target, direct))
        if t >= 2:
            mirror = fin(7 + t, (other, 2 * strip + part_half), final.at[side, slot])
            mirror.start()
            remote.append(mirror)

    for ring, base in ((ring_a3, 0), (ring_b3, TILE)):
        for h in range(2):
            proj_ref[base + 64 * h : base + 64 * h + 64, :] = ring.total(h) * scale

    pltpu.make_async_copy(final, final, r_fin.at[0]).wait()
    other, side = col // 2, lax.rem(col, 2)
    distance = lax.rem(other - strip + 8, 8)
    for h in range(2):
        straight = (distance < 4) | ((distance == 4) & (lax.rem(side + strip // 4, 2) == h))
        tile = final[h]
        over_ref[TILE * h : TILE * h + TILE, :] = jnp.where(straight, tile, tile.T) * scale

    for copy in remote:
        copy.wait_send()
    for target, copy in local:
        pl.when(target != col)(copy.wait_send)
    for copy in pairs:
        copy.wait_send()
    for ring in a_rings:
        ring.drain()

    @pl.loop(0, 4)
    def _(step):
        ring_b1(step).drain()
        ring_c1(step).drain()

    for ring in (ring_a2, ring_b2, ring_c2, ring_a3, ring_b3, ring_c3):
        ring.drain()
    rotated_store(M // CHUNK - 2).wait()
    rotated_store(M // CHUNK - 1).wait()


def local(filtered, hamiltonian_applied, rotation):
    vmem = pltpu.VMEM
    dma = pltpu.SemaphoreType.DMA
    any_spec = pl.BlockSpec(memory_space=pl.ANY)
    vmem_spec = pl.BlockSpec(memory_space=pltpu.VMEM)
    flops = 3 * 2 * ROWS * M * M * 3
    return pl.pallas_call(
        kernel,
        out_shape=(
            jax.ShapeDtypeStruct((256, TILE), F32),
            jax.ShapeDtypeStruct((256, TILE), F32),
            jax.ShapeDtypeStruct((ROWS, M), F32),
        ),
        in_specs=[any_spec] * 3,
        out_specs=(vmem_spec, vmem_spec, any_spec),
        scratch_shapes=[
            vmem((ROWS, M), F32), vmem((ROWS, M), F32), vmem((ROWS, M), F32), vmem((ROWS, M), F32),
            vmem((512, M), BF16), vmem((512, M), BF16), vmem((512, M), BF16), vmem((512, M), BF16),
            vmem((4, 256, 512), BF16), vmem((4, 256, 512), BF16),
            vmem((2, M, CHUNK), F32), vmem((2, ROWS, CHUNK), F32),
            vmem((4, 4, 4, TILE, TILE), F32), vmem((4, 4, 4, TILE, TILE), F32), vmem((4, 4, 4, BAND, TILE), F32),
            vmem((2, 6, 4, TILE, TILE), F32), vmem((4, 6, 2, TILE, TILE), F32), vmem((4, 6, 2, BAND, TILE), F32),
            vmem((4, 4, TILE, TILE), F32), vmem((4, 4, TILE, TILE), F32), vmem((4, 4, BAND, TILE), F32),
            vmem((6, 2, TILE, TILE), F32), vmem((6, 2, TILE, TILE), F32), vmem((6, 2, BAND, TILE), F32),
            vmem((4, TILE, TILE), F32), vmem((4, TILE, TILE), F32), vmem((4, BAND, TILE), F32),
            vmem((6, 64, TILE), F32), vmem((6, 64, TILE), F32), vmem((6, 72, TILE), F32),
            vmem((BAND, TILE), F32), vmem((2, TILE, TILE), F32),
            dma((2, 6)), dma((2, 6)), dma((4, 6)), dma((4, 6)), dma((4, 6)), dma((4, 6)),
            dma((3, 6)), dma((3, 6)), dma((3, 6)), dma((3, 6)),
            dma((2,)), dma((2,)), dma((16,)), dma((1,)), dma((2,)), dma((2,)), dma((2,)),
        ],
        compiler_params=pltpu.CompilerParams(
            collective_id=0, has_side_effects=True, vmem_limit_bytes=62 << 20
        ),
        cost_estimate=pl.CostEstimate(flops=flops, bytes_accessed=24 << 20, transcendentals=0),
    )(filtered, hamiltonian_applied, rotation)


def solution(mesh):
    return jax.shard_map(
        local,
        mesh=mesh,
        in_specs=(P(("row", "col"), None), P(("row", "col"), None), P()),
        out_specs=(P("row", "col"), P("row", "col"), P(("row", "col"), None)),
        check_vma=False,
    )
```

time: 427 us -> 93.5 us (0.22)
  waiting for transfers between devices: 228 us -> 0 us
  matrix products: 132 us -> 0 us
  Pallas kernels: 0 us -> 86.3 us
  blocking collectives: 35.1 us -> 0 us
  between operations: 13.8 us -> 0.64 us
  starting transfers between devices: 4.76 us -> 0 us
  local copies, waits for them, and re-layouts: 11 us -> 6.27 us
    all_gather x1 -> x0, waiting for transfers between devices: 216 us -> none  [local(): piece = lax.all_gather(psi_band, 'col', axis=1, tiled=True)]
    dot_general x3 -> x0, matrix products: 132 us -> none  [the longest x2 114 us: inner_rows(): jnp.einsum('gi,gj->ij', first, second, precision=lax.Precision.HIGHEST, p...]
    pallas_call x0 -> x1, Pallas kernels: none -> 86.3 us  [local(): pl.pallas_call(kernel, out_shape=(jax.ShapeDtypeStruct((256, TILE), F32),...]
    all_to_all x1 -> x0, blocking collectives: 35.1 us -> none  [local(): lax.all_to_all(filtered, 'col', split_axis=1, concat_axis=0, tiled=True)]
    reduce_scatter x2 -> x0, waiting for transfers between devices: 11.5 us -> none  [the longest x1 11.5 us: local(): lax.psum_scatter(proj_term, 'row', scatter_dimension=0, tiled=True)]
    all_to_all x2 -> x0, local copies, waits for them, and re-layouts: 4.69 us -> none  [the longest x1 2.88 us: local(): lax.all_to_all(hamiltonian_applied, 'col', split_axis=1, concat_axis=0, t...]
    all_to_all x1 -> x0, starting transfers between devices: 4.63 us -> none  [local(): lax.all_to_all(hamiltonian_applied, 'col', split_axis=1, concat_axis=0, t...]
  transfers between devices with their start and end apart: 4 -> 0, of which waited for: 2 -> 0; matrix products, arithmetic and copies ran while one was open for 32% -> 0% of each run, Pallas kernels for 0% -> 0%
where the time goes in v1:
time: 93.5 us; the launch traced here: 93.3 us
  Pallas kernels  86.3 us (92%)
  local copies, waits for them, and re-layouts  6.27 us (7%)
    pallas_call x1, Pallas kernels, local(): pl.pallas_call(kernel, out_shape=(jax.ShapeDtypeStruct((256, TILE), F32),...  86.3 us
    unnamed x3, local copies, waits for them, and re-layouts  6.27 us

profile of v1, /device:TPU:1, one launch (start us, length us, event | category | flops | bytes accessed | tf_op | source)
XLA Modules:
  0.0 93.3 jit_solution(7364802471747774859)
XLA Ops:
  0.6 86.3 %shard_map.58 = (f32[256,128]{1,0:T(8,128)}, f32[256,128]{1,0:T(8,128)}, f32[256,2048]{1,0:T(8,128)}) custom-call(f32[256,2048]{1,0:T(8,128)} %psi_hbm.1, f32[256,2048]{1,0:T(8,128)} %ham_hbm.1, f32[2048,2048]{1,0:T(8,128)} %rot_hbm.1), custom_call_target="tpu_custom_call" | custom-call | flops 19327352832 | bytes 25165824 | tf_op jit(solution)/shard_map/pallas_call | solution.py:407
  87.0 1.6 %copy.9 = f32[256,128]{1,0:T(8,128)} copy(f32[256,128]{1,0:T(8,128)} %get-tuple-element.6) | data formatting | bytes 262144
  88.6 1.6 %copy.10 = f32[256,128]{1,0:T(8,128)} copy(f32[256,128]{1,0:T(8,128)} %get-tuple-element.7) | data formatting | bytes 262144
  90.1 3.1 %copy.11 = f32[256,2048]{1,0:T(8,128)} copy(f32[256,2048]{1,0:T(8,128)} %get-tuple-element.8) | data formatting | bytes 4194304

commit v2 on v1

v2 whole, which is shorter than its diff:
```python
import jax
import jax.numpy as jnp
from jax import lax
from jax.experimental import pallas as pl
from jax.experimental.pallas import tpu as pltpu
from jax.sharding import PartitionSpec as P

MESH = pl.DeviceIdType.MESH
F32 = jnp.float32
BF16 = jnp.bfloat16
ROWS = 256
M = 2048
TILE = 128
BAND = 136
CUTS = ((0, 72), (72, 64))
OPENINGS = ((0, 1), (2,), (3,), ())
HALF = (0, 1, 1, 0, 0, 1)
CHUNK = 256


def split(value):
    high = value.astype(BF16)
    low = (value - high.astype(F32)).astype(BF16)
    return high, low


def dot(first, second):
    return jnp.dot(first, second, preferred_element_type=F32)


def dot3(first_high, first_low, second_high, second_low):
    first = jnp.concatenate([first_high, first_high, first_low], axis=1)
    return dot(first, jnp.concatenate([second_high, second_low, second_high], axis=0))


class Ring:
    def __init__(self, block, landing, send, recv, me, right, left):
        def copy(m):
            source, device = self.routes[m]
            return pltpu.make_async_remote_copy(
                src_ref=source,
                dst_ref=landing(m),
                send_sem=send(m),
                recv_sem=recv(m),
                device_id=device,
                device_id_type=MESH,
            )

        opposite, after, before = (lax.rem(me + n, 4) for n in (2, 1, 3))
        self.after, self.before = block(after, 0), block(before, 1)
        self.landing = landing
        self.mine = (block(me, 0), block(me, 1))
        self.copy = copy
        self.routes = (
            (block(opposite, 0), right),
            (block(opposite, 1), left),
            (block(after, 1), right),
            (block(before, 0), left),
            (self.after, right),
            (self.before, left),
        )

    def start(self, *messages):
        for m in messages:
            self.copy(m).start()

    def forward_right(self):
        self.copy(0).wait_recv()
        self.after[...] = self.after[...] + self.landing(0)[...]
        self.copy(4).start()

    def forward_left(self):
        self.copy(1).wait_recv()
        self.before[...] = self.before[...] + self.landing(1)[...]
        self.copy(5).start()

    def forward(self):
        self.forward_right()
        self.forward_left()

    def total(self, half):
        left, right = ((4, 3), (2, 5))[half]
        self.copy(left).wait_recv()
        self.copy(right).wait_recv()
        return self.mine[half][...] + self.landing(left)[...] + self.landing(right)[...]

    def drain(self):
        for m in range(6):
            self.copy(m).wait_send()


def kernel(
    psi_hbm, ham_hbm, rot_hbm, over_ref, proj_ref, rotated_hbm,
    raw_a, raw_b, pair_a, pair_b, ah, al, bh, bl, ath, atl,
    rot_buf, out_buf,
    da, db, dc, xa1, xb1, xc1, ea, eb, ec, xa2, xb2, xc2, fa, fb, fc, xa3, xb3, xc3, piece, final,
    sa1, ra1, sb1, rb1, sc1, rc1, s2, r2, s_pair, r_pair, s_fin, r_fin, load_sem, rot_sem, out_sem,
):
    row, col = lax.axis_index("row"), lax.axis_index("col")
    x, core = row // 2, lax.rem(row, 2)
    y, z = col // 4, lax.rem(col, 4)

    def chip(dx=0, dy=0, dz=0):
        return (
            2 * lax.rem(x + dx, 4) + core,
            4 * lax.rem(y + dy, 4) + lax.rem(z + dz, 4),
        )

    partner = (2 * x + 1 - core, col)
    x_right, x_left = chip(dx=1), chip(dx=3)
    y_right, y_left = chip(dy=1), chip(dy=3)
    z_right, z_left = chip(dz=1), chip(dz=3)

    load_a = pltpu.make_async_copy(psi_hbm, raw_a, load_sem.at[0])
    load_b = pltpu.make_async_copy(ham_hbm, raw_b, load_sem.at[1])
    load_a.start()
    load_b.start()
    barrier = pltpu.get_barrier_semaphore()
    for device in (partner, x_right, x_left, y_right, y_left, z_right, z_left):
        pl.semaphore_signal(barrier, inc=1, device_id=device, device_id_type=MESH)

    def rot_load(n):
        slot = lax.rem(n, 2)
        columns = pl.ds(pl.multiple_of(n * CHUNK, CHUNK), CHUNK)
        return pltpu.make_async_copy(rot_hbm.at[:, columns], rot_buf.at[slot], rot_sem.at[slot])

    def rotated_store(n):
        slot = lax.rem(n, 2)
        columns = pl.ds(pl.multiple_of(n * CHUNK, CHUNK), CHUNK)
        return pltpu.make_async_copy(out_buf.at[slot], rotated_hbm.at[:, columns], out_sem.at[slot])

    def block_of(step):
        return lax.rem(x + 2 + 3 * step + 3 * (step // 2) + 2 * (step // 3), 4)

    def cut(start, width):
        return pl.ds(pl.multiple_of(start, width), width)

    def prepare(raw, high, low, base, columns):
        h, l = split(raw[:, columns])
        high[base : base + ROWS, columns] = h
        low[base : base + ROWS, columns] = l

    load_a.wait()

    @pl.loop(0, 8)
    def _(j):
        prepare(raw_a, ah, al, 0, cut(j * 256, 256))

    load_b.wait()

    @pl.loop(0, 4)
    def _(j):
        prepare(raw_b, bh, bl, 0, cut(j * 512, 512))

    pl.semaphore_wait(barrier, 7)

    y_order = (2, 1, 3, 0)

    def pair_copy(source, target, columns, n):
        return pltpu.make_async_remote_copy(
            src_ref=source.at[:, columns],
            dst_ref=target.at[:, columns],
            send_sem=s_pair.at[n],
            recv_sem=r_pair.at[n],
            device_id=partner,
            device_id_type=MESH,
        )

    def a_columns(first, j):
        return cut(lax.rem(first + j, 8) * 256, 256)

    def b_columns(i):
        return cut(lax.rem(y + y_order[i], 4) * 512, 512)

    def pair_a_copy(first, j):
        return pair_copy(psi_hbm, pair_a, a_columns(first, j), j)

    def pair_b_copy(i):
        return pair_copy(ham_hbm, pair_b, b_columns(i), 8 + i)

    first = 2 * block_of(0) + core
    theirs = 2 * block_of(0) + 1 - core
    pair_a_copy(theirs, 0).start()
    pair_a_copy(theirs, 4).start()
    pair_b_copy(0).start()
    for j in (1, 2, 3):
        pair_a_copy(theirs, j).start()
    for i in (1, 2, 3):
        pair_b_copy(i).start()
    for j in (5, 6, 7):
        pair_a_copy(theirs, j).start()
    rot_load(0).start()
    rot_load(1).start()

    def take_a(j):
        pair_a_copy(first, j).wait_recv()
        prepare(pair_a, ah, al, ROWS, a_columns(first, j))

    def take_b(i):
        pair_b_copy(i).wait_recv()
        prepare(pair_b, bh, bl, ROWS, b_columns(i))

    def turn(columns):
        for raw, base in ((raw_a, 0), (pair_a, ROWS)):
            h, l = split(raw[:, columns].T)
            ath[:, base : base + ROWS] = h
            atl[:, base : base + ROWS] = l

    def rotated_chunk(n):
        slot = lax.rem(n, 2)
        rot_load(n).wait()
        acc = jnp.zeros((ROWS, CHUNK), F32)
        for k in range(8):
            h, l = split(rot_buf[slot, 256 * k : 256 * k + 256, :])
            part = slice(256 * k, 256 * k + 256)
            acc = acc + dot3(ah[0:ROWS, part], al[0:ROWS, part], h, l)

        @pl.when(n >= 2)
        def _():
            rotated_store(n - 2).wait()

        out_buf[slot] = acc
        rotated_store(n).start()

        @pl.when(n + 2 < M // CHUNK)
        def _():
            rot_load(n + 2).start()

    y_off = ((2, 1), (3, 0))

    def ring_a1(s):
        return Ring(
            lambda u, h: da.at[u, lax.rem(y + y_off[s][h], 4)],
            lambda m: xa1.at[s, m],
            lambda m: sa1.at[s, m],
            lambda m: ra1.at[s, m],
            x, x_right, x_left,
        )

    def ring_b1(step):
        block = block_of(step)
        return Ring(
            lambda u, h: db.at[block, u, 2 * h : 2 * h + 2],
            lambda m: xb1.at[step, m],
            lambda m: sb1.at[step, m],
            lambda m: rb1.at[step, m],
            y, y_right, y_left,
        )

    def ring_c1(step):
        block = block_of(step)
        return Ring(
            lambda u, h: dc.at[block, u, 2 * h : 2 * h + 2],
            lambda m: xc1.at[step, m],
            lambda m: sc1.at[step, m],
            lambda m: rc1.at[step, m],
            z, z_right, z_left,
        )

    a_rings = [ring_a1(0), ring_a1(1)]

    @pl.loop(0, 4)
    def _(step):
        block = block_of(step)
        strip = 2 * block + core
        b_ring, c_ring = ring_b1(step), ring_c1(step)
        opening = step == 0

        def at_opening(*takes):
            @pl.when(opening)
            def _():
                for take, n in takes:
                    take(n)

        def square(j):
            columns = a_columns(strip, j)
            return dot3(ath[...], atl[...], ah[:, columns], al[:, columns])

        def projected(i):
            yy = lax.rem(y + y_order[i], 4)
            columns = b_columns(i)
            acc = dot3(ath[...], atl[...], bh[:, columns], bl[:, columns])
            for t in range(4):
                da[block, yy, t, 0:TILE] = acc[0:TILE, TILE * t : TILE * t + TILE]
                db[block, yy, t, 0:TILE] = acc[TILE:ROWS, TILE * t : TILE * t + TILE]
            s, h = i // 2, i % 2

            @pl.when(step == 0)
            def _():
                a_rings[s].start(h)

            @pl.when(step == 2 - h)
            def _():
                a_rings[s].start(3 - h)

        at_opening((take_a, 0))
        turn(a_columns(strip, 0))
        at_opening((take_a, 4))
        acc = square(4)
        swap = strip >= 4
        top = jnp.where(swap, acc[0:TILE, TILE:256], acc[0:TILE, 0:TILE]).reshape(2, 4, 16, TILE)
        low = jnp.where(swap, acc[TILE:ROWS, 0:TILE], acc[TILE:ROWS, TILE:256]).reshape(2, 4, 16, TILE)
        for zz in range(4):
            tile = (top, low)[zz // 2][zz % 2]
            da[block, :, zz, TILE:BAND, :] = tile[:, 0:8]
            db[block, :, zz, TILE:BAND, :] = tile[:, 8:16]
        at_opening((take_b, 0))
        projected(0)
        b_ring.start(0, 1)
        at_opening((take_a, 1), (take_a, 2), (take_a, 3))
        for j in range(4):
            acc = square(j)
            for h in range(2):
                t = 2 * j + h
                tile = acc[:, TILE * h : TILE * h + TILE].reshape(4, 4, 16, TILE)
                dc[block, :, :, 16 * t : 16 * t + 16, :] = tile
        c_ring.start(0, 1, 2, 3)
        at_opening((take_b, 1))
        projected(1)
        b_ring.start(2)
        at_opening((take_b, 2))
        projected(2)
        b_ring.start(3)
        at_opening((take_b, 3))
        projected(3)
        at_opening((take_a, 5), (take_a, 6), (take_a, 7))

        @pl.when(step >= 1)
        def _():
            ring_c1(step - 1).forward()
            ring_b1(step - 1).forward()

        @pl.when(step == 2)
        def _():
            a_rings[0].forward()

    def ring_n(block, landing, sems, me, right, left):
        send, recv = sems
        return Ring(block, landing, lambda m: send.at[m], lambda m: recv.at[m], me, right, left)

    def sems(n):
        return s2.at[n], r2.at[n]

    def in_band(ref, *index):
        return lambda u, h: ref.at[(*index, u, pl.ds(*CUTS[h]))]

    def band_landing(ref, *index):
        return lambda m: ref.at[(*index, m, pl.ds(0, CUTS[HALF[m]][1]))]

    ring_a2 = ring_n(lambda u, h: ea.at[u, 2 * h : 2 * h + 2], lambda m: xa2.at[m], sems(0), y, y_right, y_left)
    ring_c2 = ring_n(lambda u, h: ec.at[u, 2 * h : 2 * h + 2], lambda m: xc2.at[m], sems(1), x, x_right, x_left)
    b2_rings = [
        ring_n(in_band(eb, n), band_landing(xb2, n), sems(2 + n), z, z_right, z_left) for n in range(4)
    ]
    ring_a3 = ring_n(in_band(fa), band_landing(xa3), sems(6), z, z_right, z_left)
    ring_b3 = ring_n(in_band(fb), band_landing(xb3), sems(7), x, x_right, x_left)
    ring_c3 = ring_n(
        lambda u, h: fc.at[u, 64 * h : 64 * h + 64], lambda m: xc3.at[m], sems(8), y, y_right, y_left
    )

    def total_b1(n):
        ring = ring_b1(n)
        for h in range(2):
            eb[n, 2 * h : 2 * h + 2] = ring.total(h)
        b2_rings[n].start(0, 1, 2, 3)

    def total_c1(n):
        ring = ring_c1(n)
        for h in range(2):
            ec[block_of(n), 2 * h : 2 * h + 2] = ring.total(h)
        ring_c2.start(*OPENINGS[n])

    def total_a1(s, h):
        ea[lax.rem(y + y_off[s][h], 4)] = a_rings[s].total(h)
        ring_a2.start(*OPENINGS[2 * s + h])

    def total_b2(n):
        for h in range(2):
            start, size = CUTS[h]
            fb[block_of(n), start : start + size] = b2_rings[n].total(h)
        ring_b3.start(*OPENINGS[n])

    def total_2(ring, ref, then):
        for h in range(2):
            ref[2 * h : 2 * h + 2] = ring.total(h)
        then.start(0, 1, 2, 3)

    def total_c3():
        for h in range(2):
            piece[64 * h : 64 * h + 64] = ring_c3.total(h)
        for finish in finishes[:8]:
            finish.start()

    def total_3(ring, base, rest):
        head, tail = ring.total(0), ring.total(1)
        proj_ref[base : base + 72, :] = head * scale
        proj_ref[base + 72 : base + TILE, :] = tail[0:56] * scale
        piece[rest : rest + 8] = tail[56:64]

    scale = 1.0 / (ROWS * 128)
    strip = row
    part = 4 * z + y
    part_half, part_rest = part // 8, lax.rem(part, 8)
    slot = pl.ds(pl.multiple_of(16 * part_rest, 16), 16)

    class Finish:
        def __init__(self, t):
            self.t, self.source = t, piece.at[16 * t : 16 * t + 16]
            self.other = lax.rem(strip + t // 2, 8)
            self.side = t % 2 if t < 8 else lax.rem(part_half + strip // 4, 2)
            self.target = 2 * self.other + self.side

        def copy(self, n, device, place):
            return pltpu.make_async_remote_copy(
                src_ref=self.source,
                dst_ref=place,
                send_sem=s_fin.at[n],
                recv_sem=r_fin.at[0],
                device_id=device,
                device_id_type=MESH,
            )

        def direct(self):
            return self.copy(self.t, (strip, self.target), final.at[part_half, slot])

        def mirror(self):
            return self.copy(7 + self.t, (self.other, 2 * strip + part_half), final.at[self.side, slot])

        def start(self):
            stay = pltpu.make_async_copy(self.source, final.at[part_half, slot], r_fin.at[0])
            direct = self.direct()
            pl.when(self.target != col)(direct.start)
            pl.when(self.target == col)(stay.start)
            if self.t >= 2:
                self.mirror().start()

        def drain(self):
            pl.when(self.target != col)(self.direct().wait_send)
            if self.t >= 2:
                self.mirror().wait_send()

    finishes = [Finish(t) for t in range(9)]

    a_rings[1].forward_right()
    total_b1(0)
    total_c1(0)
    a_rings[1].forward_left()
    pl.loop(0, 2)(rotated_chunk)
    total_c1(1)
    total_b1(1)
    pl.loop(2, 3)(rotated_chunk)
    ring_c1(3).forward_left()
    ring_b1(3).forward_right()
    ring_c1(3).forward_right()
    ring_b1(3).forward_left()
    pl.loop(3, 4)(rotated_chunk)
    total_a1(0, 0)
    pl.loop(4, 6)(rotated_chunk)
    total_b1(2)
    total_c1(2)
    b2_rings[0].forward_right()
    b2_rings[1].forward_left()
    b2_rings[1].forward_right()
    ring_c2.forward_left()
    b2_rings[0].forward_left()
    total_a1(1, 0)
    total_b1(3)
    total_a1(0, 1)
    pl.loop(6, 7)(rotated_chunk)
    b2_rings[2].forward_right()
    ring_a2.forward_right()
    b2_rings[2].forward_left()
    ring_a2.forward_left()
    ring_c2.forward_right()
    total_c1(3)
    pl.loop(7, 8)(rotated_chunk)
    b2_rings[3].forward_left()
    b2_rings[3].forward_right()
    total_b2(0)
    total_b2(1)
    total_a1(1, 1)
    total_b2(2)
    total_b2(3)
    total_2(ring_a2, fa, ring_a3)
    total_2(ring_c2, fc, ring_c3)
    ring_b3.forward_left()
    ring_b3.forward_right()
    ring_a3.forward_left()
    ring_a3.forward_right()
    ring_c3.forward_right()
    ring_c3.forward_left()
    total_3(ring_b3, TILE, 136)
    total_3(ring_a3, 0, 128)
    finishes[8].start()
    total_c3()

    for n in range(12):
        (pair_a_copy(theirs, n) if n < 8 else pair_b_copy(n - 8)).wait_send()
    for ring in a_rings:
        ring.drain()

    @pl.loop(0, 4)
    def _(step):
        ring_b1(step).drain()
        ring_c1(step).drain()

    for ring in (ring_a2, ring_c2, *b2_rings, ring_a3, ring_b3, ring_c3):
        ring.drain()
    rotated_store(M // CHUNK - 2).wait()
    rotated_store(M // CHUNK - 1).wait()

    pltpu.make_async_copy(final, final, r_fin.at[0]).wait()
    other, side = col // 2, lax.rem(col, 2)
    distance = lax.rem(other - strip + 8, 8)
    for h in range(2):
        straight = (distance < 4) | ((distance == 4) & (lax.rem(side + strip // 4, 2) == h))
        tile = final[h]
        over_ref[TILE * h : TILE * h + TILE, :] = jnp.where(straight, tile, tile.T) * scale
    for finish in finishes:
        finish.drain()


def hand_on(over_in, proj_in, rotated_in, over_out, proj_out, rotated_out, over, proj, rotated, load, store):
    moves = [(over_in, over, over_out), (proj_in, proj, proj_out)]
    for n in range(4):
        rows = pl.ds(64 * n, 64)
        moves.append((rotated_in.at[rows], rotated.at[rows], rotated_out.at[rows]))
    loads = [pltpu.make_async_copy(a, b, load.at[n]) for n, (a, b, _) in enumerate(moves)]
    stores = [pltpu.make_async_copy(b, c, store.at[n]) for n, (_, b, c) in enumerate(moves)]
    for copy in loads:
        copy.start()
    for first, second in zip(loads, stores):
        first.wait()
        second.start()
    for copy in stores:
        copy.wait()


def local(filtered, hamiltonian_applied, rotation):
    vmem = pltpu.VMEM
    dma = pltpu.SemaphoreType.DMA
    any_spec = pl.BlockSpec(memory_space=pl.ANY)
    vmem_spec = pl.BlockSpec(memory_space=pltpu.VMEM)
    flops = 3 * 2 * ROWS * M * M * 3
    shapes = (
        jax.ShapeDtypeStruct((256, TILE), F32),
        jax.ShapeDtypeStruct((256, TILE), F32),
        jax.ShapeDtypeStruct((ROWS, M), F32),
    )
    made = pl.pallas_call(
        kernel,
        out_shape=shapes,
        in_specs=[any_spec] * 3,
        out_specs=(vmem_spec, vmem_spec, any_spec),
        scratch_shapes=[
            vmem((ROWS, M), F32), vmem((ROWS, M), F32), vmem((ROWS, M), F32), vmem((ROWS, M), F32),
            vmem((512, M), BF16), vmem((512, M), BF16), vmem((512, M), BF16), vmem((512, M), BF16),
            vmem((256, 512), BF16), vmem((256, 512), BF16),
            vmem((2, M, CHUNK), F32), vmem((2, ROWS, CHUNK), F32),
            vmem((4, 4, 4, BAND, TILE), F32), vmem((4, 4, 4, BAND, TILE), F32), vmem((4, 4, 4, TILE, TILE), F32),
            vmem((2, 6, 4, BAND, TILE), F32), vmem((4, 6, 2, BAND, TILE), F32), vmem((4, 6, 2, TILE, TILE), F32),
            vmem((4, 4, BAND, TILE), F32), vmem((4, 4, BAND, TILE), F32), vmem((4, 4, TILE, TILE), F32),
            vmem((6, 2, BAND, TILE), F32), vmem((4, 6, 72, TILE), F32), vmem((6, 2, TILE, TILE), F32),
            vmem((4, BAND, TILE), F32), vmem((4, BAND, TILE), F32), vmem((4, TILE, TILE), F32),
            vmem((6, 72, TILE), F32), vmem((6, 72, TILE), F32), vmem((6, 64, TILE), F32),
            vmem((144, TILE), F32), vmem((2, TILE, TILE), F32),
            dma((2, 6)), dma((2, 6)), dma((4, 6)), dma((4, 6)), dma((4, 6)), dma((4, 6)),
            dma((9, 6)), dma((9, 6)),
            dma((12,)), dma((12,)), dma((16,)), dma((1,)), dma((2,)), dma((2,)), dma((2,)),
        ],
        compiler_params=pltpu.CompilerParams(
            collective_id=0, has_side_effects=True, vmem_limit_bytes=62 << 20
        ),
        cost_estimate=pl.CostEstimate(flops=flops, bytes_accessed=24 << 20, transcendentals=0),
    )(filtered, hamiltonian_applied, rotation)
    return pl.pallas_call(
        hand_on,
        out_shape=shapes,
        in_specs=[any_spec] * 3,
        out_specs=(any_spec,) * 3,
        scratch_shapes=[vmem((256, TILE), F32), vmem((256, TILE), F32), vmem((ROWS, M), F32), dma((6,)), dma((6,))],
    )(*made)


def solution(mesh):
    return jax.shard_map(
        local,
        mesh=mesh,
        in_specs=(P(("row", "col"), None), P(("row", "col"), None), P()),
        out_specs=(P("row", "col"), P("row", "col"), P(("row", "col"), None)),
        check_vma=False,
    )
```

time: 93.5 us -> 77.1 us (0.82)
  Pallas kernels: 86.3 us -> 76.3 us
  local copies, waits for them, and re-layouts: 6.27 us -> 0 us
    pallas_call x1 -> x2, Pallas kernels: 86.3 us -> 76.3 us  [the longest x1 73.7 us: local(): pl.pallas_call(kernel, out_shape=shapes, in_specs=[any_spec] * 3, out_spe...]
    unnamed x3 -> x0, local copies, waits for them, and re-layouts: 6.27 us -> none
where the time goes in v2:
time: 77.1 us; the launch traced here: 76.9 us
  Pallas kernels  76.3 us (99%)
    pallas_call x1, Pallas kernels, local(): pl.pallas_call(kernel, out_shape=shapes, in_specs=[any_spec] * 3, out_spe...  73.7 us
    pallas_call x1, Pallas kernels, local(): pl.pallas_call(hand_on, out_shape=shapes, in_specs=[any_spec] * 3, out_sp...  2.59 us

profile of v2, /device:TPU:1, one launch (start us, length us, event | category | flops | bytes accessed | tf_op | source)
XLA Modules:
  0.0 76.9 jit_solution(9348223497544039626)
XLA Ops:
  0.6 73.7 %shard_map.58 = (f32[256,128]{1,0:T(8,128)}, f32[256,128]{1,0:T(8,128)}, f32[256,2048]{1,0:T(8,128)}) custom-call(f32[256,2048]{1,0:T(8,128)} %psi_hbm.1, f32[256,2048]{1,0:T(8,128)} %ham_hbm.1, f32[2048,2048]{1,0:T(8,128)} %rot_hbm.1), custom_call_target="tpu_custom_call" | custom-call | flops 19327352832 | bytes 25165824 | tf_op jit(solution)/shard_map/pallas_call | solution.py:550
  74.3 2.6 %shard_map.59 = (f32[256,128]{1,0:T(8,128)}, f32[256,128]{1,0:T(8,128)}, f32[256,2048]{1,0:T(8,128)}) custom-call(f32[256,128]{1,0:T(8,128)} %get-tuple-element.6.over_in, f32[256,128]{1,0:T(8,128)} %get-tuple-element.7.proj_in, f32[256,2048]{1,0:T(8,128)} %get-tuple-element.8.rotated_in), custom_call_target="tpu_custom_call" | custom-call | tf_op jit(solution)/shard_map/pallas_call | solution.py:576

commit v3 on v2

--- a/solution.py
+++ b/solution.py
@@ -89,11 +89,41 @@
             self.copy(m).wait_send()
 
 
+class Direct:
+    def __init__(self, block, landing, send, recv, me, devices):
+        self.mine, self.landing = block(me), landing
+
+        def copy(m):
+            return pltpu.make_async_remote_copy(
+                src_ref=block(lax.rem(me + (1, 3, 2)[m], 4)),
+                dst_ref=landing(m),
+                send_sem=send(m),
+                recv_sem=recv(m),
+                device_id=devices[m],
+                device_id_type=MESH,
+            )
+
+        self.copy = copy
+
+    def start(self, *messages):
+        for m in messages:
+            self.copy(m).start()
+
+    def total(self):
+        for m in range(3):
+            self.copy(m).wait_recv()
+        return (self.mine[...] + self.landing(0)[...]) + (self.landing(1)[...] + self.landing(2)[...])
+
+    def drain(self):
+        for m in range(3):
+            self.copy(m).wait_send()
+
+
 def kernel(
     psi_hbm, ham_hbm, rot_hbm, over_ref, proj_ref, rotated_hbm,
     raw_a, raw_b, pair_a, pair_b, ah, al, bh, bl, ath, atl,
     rot_buf, out_buf,
-    da, db, dc, xa1, xb1, xc1, ea, eb, ec, xa2, xb2, xc2, fa, fb, fc, xa3, xb3, xc3, piece, final,
+    da, db, dc, xa1, xb1, xc1, ea, eb, ec, xa2, xb2, xb2_last, xc2, fa, fb, fc, xa3, xb3, xc3, piece, final,
     sa1, ra1, sb1, rb1, sc1, rc1, s2, r2, s_pair, r_pair, s_fin, r_fin, load_sem, rot_sem, out_sem,
 ):
     row, col = lax.axis_index("row"), lax.axis_index("col")
@@ -183,9 +213,10 @@
     pair_a_copy(theirs, 0).start()
     pair_a_copy(theirs, 4).start()
     pair_b_copy(0).start()
+    pair_b_copy(1).start()
     for j in (1, 2, 3):
         pair_a_copy(theirs, j).start()
-    for i in (1, 2, 3):
+    for i in (2, 3):
         pair_b_copy(i).start()
     for j in (5, 6, 7):
         pair_a_copy(theirs, j).start()
@@ -228,12 +259,13 @@
 
     y_off = ((2, 1), (3, 0))
 
-    def ring_a1(s):
+    def ring_a1(n):
+        s, pair = n // 2, n % 2
         return Ring(
-            lambda u, h: da.at[u, lax.rem(y + y_off[s][h], 4)],
-            lambda m: xa1.at[s, m],
-            lambda m: sa1.at[s, m],
-            lambda m: ra1.at[s, m],
+            lambda u, h: da.at[u, lax.rem(y + y_off[s][h], 4), 2 * pair : 2 * pair + 2],
+            lambda m: xa1.at[n, m],
+            lambda m: sa1.at[n, m],
+            lambda m: ra1.at[n, m],
             x, x_right, x_left,
         )
 
@@ -257,7 +289,7 @@
             z, z_right, z_left,
         )
 
-    a_rings = [ring_a1(0), ring_a1(1)]
+    a_rings = [ring_a1(n) for n in range(4)]
 
     @pl.loop(0, 4)
     def _(step):
@@ -287,11 +319,13 @@
 
             @pl.when(step == 0)
             def _():
-                a_rings[s].start(h)
+                for ring in a_rings[2 * s : 2 * s + 2]:
+                    ring.start(h)
 
             @pl.when(step == 2 - h)
             def _():
-                a_rings[s].start(3 - h)
+                for ring in a_rings[2 * s : 2 * s + 2]:
+                    ring.start(3 - h)
 
         at_opening((take_a, 0))
         turn(a_columns(strip, 0))
@@ -307,6 +341,9 @@
         at_opening((take_b, 0))
         projected(0)
         b_ring.start(0, 1)
+        at_opening((take_b, 1))
+        projected(1)
+        b_ring.start(2)
         at_opening((take_a, 1), (take_a, 2), (take_a, 3))
         for j in range(4):
             acc = square(j)
@@ -315,9 +352,6 @@
                 tile = acc[:, TILE * h : TILE * h + TILE].reshape(4, 4, 16, TILE)
                 dc[block, :, :, 16 * t : 16 * t + 16, :] = tile
         c_ring.start(0, 1, 2, 3)
-        at_opening((take_b, 1))
-        projected(1)
-        b_ring.start(2)
         at_opening((take_b, 2))
         projected(2)
         b_ring.start(3)
@@ -333,6 +367,7 @@
         @pl.when(step == 2)
         def _():
             a_rings[0].forward()
+            a_rings[1].forward()
 
     def ring_n(block, landing, sems, me, right, left):
         send, recv = sems
@@ -350,19 +385,28 @@
     ring_a2 = ring_n(lambda u, h: ea.at[u, 2 * h : 2 * h + 2], lambda m: xa2.at[m], sems(0), y, y_right, y_left)
     ring_c2 = ring_n(lambda u, h: ec.at[u, 2 * h : 2 * h + 2], lambda m: xc2.at[m], sems(1), x, x_right, x_left)
     b2_rings = [
-        ring_n(in_band(eb, n), band_landing(xb2, n), sems(2 + n), z, z_right, z_left) for n in range(4)
+        ring_n(in_band(eb, n), band_landing(xb2, n), sems(2 + n), z, z_right, z_left) for n in range(3)
     ]
-    ring_a3 = ring_n(in_band(fa), band_landing(xa3), sems(6), z, z_right, z_left)
-    ring_b3 = ring_n(in_band(fb), band_landing(xb3), sems(7), x, x_right, x_left)
-    ring_c3 = ring_n(
-        lambda u, h: fc.at[u, 64 * h : 64 * h + 64], lambda m: xc3.at[m], sems(8), y, y_right, y_left
-    )
+
+    def direct_n(block, landing, n, me, devices):
+        return Direct(block, lambda m: landing.at[m], lambda m: s2.at[n, m], lambda m: r2.at[n, m], me, devices)
+
+    x_devices = (x_right, x_left, chip(dx=2))
+    y_devices = (y_right, y_left, chip(dy=2))
+    z_devices = (z_right, z_left, chip(dz=2))
+    b2_last = direct_n(lambda u: eb.at[3, u], xb2_last, 5, z, z_devices)
+    ring_a3 = direct_n(lambda u: fa.at[u], xa3, 6, z, z_devices)
+    ring_b3 = direct_n(lambda u: fb.at[u], xb3, 7, x, x_devices)
+    ring_c3 = direct_n(lambda u: fc.at[u], xc3, 8, y, y_devices)
 
     def total_b1(n):
         ring = ring_b1(n)
         for h in range(2):
             eb[n, 2 * h : 2 * h + 2] = ring.total(h)
-        b2_rings[n].start(0, 1, 2, 3)
+        if n < 3:
+            b2_rings[n].start(0, 1, 2, 3)
+        else:
+            b2_last.start(2, 0, 1)
 
     def total_c1(n):
         ring = ring_c1(n)
@@ -371,31 +415,33 @@
         ring_c2.start(*OPENINGS[n])
 
     def total_a1(s, h):
-        ea[lax.rem(y + y_off[s][h], 4)] = a_rings[s].total(h)
+        for n in range(2):
+            ea[lax.rem(y + y_off[s][h], 4), 2 * n : 2 * n + 2] = a_rings[2 * s + n].total(h)
         ring_a2.start(*OPENINGS[2 * s + h])
 
     def total_b2(n):
+        if n == 3:
+            fb[block_of(n)] = b2_last.total()
+            return
         for h in range(2):
             start, size = CUTS[h]
             fb[block_of(n), start : start + size] = b2_rings[n].total(h)
-        ring_b3.start(*OPENINGS[n])
+        ring_b3.start((2, 0, 1)[n])
 
     def total_2(ring, ref, then):
         for h in range(2):
             ref[2 * h : 2 * h + 2] = ring.total(h)
-        then.start(0, 1, 2, 3)
+        then.start(2, 0, 1)
 
     def total_c3():
-        for h in range(2):
-            piece[64 * h : 64 * h + 64] = ring_c3.total(h)
+        piece[0:TILE] = ring_c3.total()
         for finish in finishes[:8]:
             finish.start()
 
     def total_3(ring, base, rest):
-        head, tail = ring.total(0), ring.total(1)
-        proj_ref[base : base + 72, :] = head * scale
-        proj_ref[base + 72 : base + TILE, :] = tail[0:56] * scale
-        piece[rest : rest + 8] = tail[56:64]
+        total = ring.total()
+        proj_ref[base : base + TILE, :] = total[0:TILE] * scale
+        piece[rest : rest + 8] = total[TILE:BAND]
 
     scale = 1.0 / (ROWS * 128)
     strip = row
@@ -441,58 +487,51 @@
 
     finishes = [Finish(t) for t in range(9)]
 
-    a_rings[1].forward_right()
-    total_b1(0)
+    a_rings[2].forward_right()
+    a_rings[3].forward_right()
     total_c1(0)
-    a_rings[1].forward_left()
-    pl.loop(0, 2)(rotated_chunk)
+    pl.loop(0, 3)(rotated_chunk)
     total_c1(1)
-    total_b1(1)
-    pl.loop(2, 3)(rotated_chunk)
-    ring_c1(3).forward_left()
+    pl.loop(3, 4)(rotated_chunk)
+    ring_b1(3).forward_left()
     ring_b1(3).forward_right()
     ring_c1(3).forward_right()
-    ring_b1(3).forward_left()
-    pl.loop(3, 4)(rotated_chunk)
+    a_rings[3].forward_left()
+    total_b1(0)
+    ring_c1(3).forward_left()
     total_a1(0, 0)
+    total_a1(0, 1)
     pl.loop(4, 6)(rotated_chunk)
+    total_c1(2)
     total_b1(2)
-    total_c1(2)
+    ring_c2.forward_left()
+    a_rings[2].forward_left()
+    total_b1(1)
+    b2_rings[0].forward_left()
+    total_a1(1, 0)
+    pl.loop(6, 7)(rotated_chunk)
     b2_rings[0].forward_right()
+    ring_c2.forward_right()
+    b2_rings[2].forward_left()
+    ring_a2.forward_left()
+    ring_a2.forward_right()
+    b2_rings[2].forward_right()
+    total_c1(3)
     b2_rings[1].forward_left()
     b2_rings[1].forward_right()
-    ring_c2.forward_left()
-    b2_rings[0].forward_left()
-    total_a1(1, 0)
     total_b1(3)
-    total_a1(0, 1)
-    pl.loop(6, 7)(rotated_chunk)
-    b2_rings[2].forward_right()
-    ring_a2.forward_right()
-    b2_rings[2].forward_left()
-    ring_a2.forward_left()
-    ring_c2.forward_right()
-    total_c1(3)
     pl.loop(7, 8)(rotated_chunk)
-    b2_rings[3].forward_left()
-    b2_rings[3].forward_right()
+    total_b2(2)
     total_b2(0)
     total_b2(1)
+    total_2(ring_c2, fc, ring_c3)
     total_a1(1, 1)
-    total_b2(2)
+    total_2(ring_a2, fa, ring_a3)
     total_b2(3)
-    total_2(ring_a2, fa, ring_a3)
-    total_2(ring_c2, fc, ring_c3)
-    ring_b3.forward_left()
-    ring_b3.forward_right()
-    ring_a3.forward_left()
-    ring_a3.forward_right()
-    ring_c3.forward_right()
-    ring_c3.forward_left()
     total_3(ring_b3, TILE, 136)
+    total_c3()
     total_3(ring_a3, 0, 128)
     finishes[8].start()
-    total_c3()
 
     for n in range(12):
         (pair_a_copy(theirs, n) if n < 8 else pair_b_copy(n - 8)).wait_send()
@@ -504,7 +543,7 @@
         ring_b1(step).drain()
         ring_c1(step).drain()
 
-    for ring in (ring_a2, ring_c2, *b2_rings, ring_a3, ring_b3, ring_c3):
+    for ring in (ring_a2, ring_c2, *b2_rings, b2_last, ring_a3, ring_b3, ring_c3):
         ring.drain()
     rotated_store(M // CHUNK - 2).wait()
     rotated_store(M // CHUNK - 1).wait()
@@ -558,13 +597,13 @@
             vmem((256, 512), BF16), vmem((256, 512), BF16),
             vmem((2, M, CHUNK), F32), vmem((2, ROWS, CHUNK), F32),
             vmem((4, 4, 4, BAND, TILE), F32), vmem((4, 4, 4, BAND, TILE), F32), vmem((4, 4, 4, TILE, TILE), F32),
-            vmem((2, 6, 4, BAND, TILE), F32), vmem((4, 6, 2, BAND, TILE), F32), vmem((4, 6, 2, TILE, TILE), F32),
+            vmem((4, 6, 2, BAND, TILE), F32), vmem((4, 6, 2, BAND, TILE), F32), vmem((4, 6, 2, TILE, TILE), F32),
             vmem((4, 4, BAND, TILE), F32), vmem((4, 4, BAND, TILE), F32), vmem((4, 4, TILE, TILE), F32),
-            vmem((6, 2, BAND, TILE), F32), vmem((4, 6, 72, TILE), F32), vmem((6, 2, TILE, TILE), F32),
+            vmem((6, 2, BAND, TILE), F32), vmem((3, 6, 72, TILE), F32), vmem((3, BAND, TILE), F32), vmem((6, 2, TILE, TILE), F32),
             vmem((4, BAND, TILE), F32), vmem((4, BAND, TILE), F32), vmem((4, TILE, TILE), F32),
-            vmem((6, 72, TILE), F32), vmem((6, 72, TILE), F32), vmem((6, 64, TILE), F32),
+            vmem((3, BAND, TILE), F32), vmem((3, BAND, TILE), F32), vmem((3, TILE, TILE), F32),
             vmem((144, TILE), F32), vmem((2, TILE, TILE), F32),
-            dma((2, 6)), dma((2, 6)), dma((4, 6)), dma((4, 6)), dma((4, 6)), dma((4, 6)),
+            dma((4, 6)), dma((4, 6)), dma((4, 6)), dma((4, 6)), dma((4, 6)), dma((4, 6)),
             dma((9, 6)), dma((9, 6)),
             dma((12,)), dma((12,)), dma((16,)), dma((1,)), dma((2,)), dma((2,)), dma((2,)),
         ],

time: 77.1 us -> 74.7 us (0.969)
  Pallas kernels: 76.3 us -> 73.9 us
    pallas_call x1, Pallas kernels: 73.7 us -> 71.3 us  [local(): pl.pallas_call(kernel, out_shape=shapes, in_specs=[any_spec] * 3, out_spe...]
where the time goes in v3:
time: 74.7 us; the launch traced here: 74.5 us
  Pallas kernels  73.9 us (99%)
    pallas_call x1, Pallas kernels, local(): pl.pallas_call(kernel, out_shape=shapes, in_specs=[any_spec] * 3, out_spe...  71.3 us
    pallas_call x1, Pallas kernels, local(): pl.pallas_call(hand_on, out_shape=shapes, in_specs=[any_spec] * 3, out_sp...  2.59 us

profile of v3, /device:TPU:1, one launch (start us, length us, event | category | flops | bytes accessed | tf_op | source)
XLA Modules:
  0.0 74.5 jit_solution(1397248086306599972)
XLA Ops:
  0.6 71.3 %shard_map.58 = (f32[256,128]{1,0:T(8,128)}, f32[256,128]{1,0:T(8,128)}, f32[256,2048]{1,0:T(8,128)}) custom-call(f32[256,2048]{1,0:T(8,128)} %psi_hbm.1, f32[256,2048]{1,0:T(8,128)} %ham_hbm.1, f32[2048,2048]{1,0:T(8,128)} %rot_hbm.1), custom_call_target="tpu_custom_call" | custom-call | flops 19327352832 | bytes 25165824 | tf_op jit(solution)/shard_map/pallas_call | solution.py:589
  71.9 2.6 %shard_map.59 = (f32[256,128]{1,0:T(8,128)}, f32[256,128]{1,0:T(8,128)}, f32[256,2048]{1,0:T(8,128)}) custom-call(f32[256,128]{1,0:T(8,128)} %get-tuple-element.6.over_in, f32[256,128]{1,0:T(8,128)} %get-tuple-element.7.proj_in, f32[256,2048]{1,0:T(8,128)} %get-tuple-element.8.rotated_in), custom_call_target="tpu_custom_call" | custom-call | tf_op jit(solution)/shard_map/pallas_call | solution.py:615

commit v4 on v3

--- a/solution.py
+++ b/solution.py
@@ -492,39 +492,39 @@
     total_c1(0)
     pl.loop(0, 3)(rotated_chunk)
     total_c1(1)
-    pl.loop(3, 4)(rotated_chunk)
-    ring_b1(3).forward_left()
+    a_rings[2].forward_left()
     ring_b1(3).forward_right()
+    total_b1(1)
     ring_c1(3).forward_right()
-    a_rings[3].forward_left()
     total_b1(0)
     ring_c1(3).forward_left()
     total_a1(0, 0)
+    ring_b1(3).forward_left()
     total_a1(0, 1)
-    pl.loop(4, 6)(rotated_chunk)
+    pl.loop(3, 5)(rotated_chunk)
     total_c1(2)
+    b2_rings[1].forward_right()
+    b2_rings[1].forward_left()
+    ring_c2.forward_left()
+    a_rings[3].forward_left()
     total_b1(2)
-    ring_c2.forward_left()
-    a_rings[2].forward_left()
-    total_b1(1)
+    total_a1(1, 0)
     b2_rings[0].forward_left()
-    total_a1(1, 0)
+    ring_a2.forward_left()
+    pl.loop(5, 6)(rotated_chunk)
+    ring_c2.forward_right()
+    b2_rings[0].forward_right()
+    ring_a2.forward_right()
     pl.loop(6, 7)(rotated_chunk)
-    b2_rings[0].forward_right()
-    ring_c2.forward_right()
+    total_c1(3)
     b2_rings[2].forward_left()
-    ring_a2.forward_left()
-    ring_a2.forward_right()
     b2_rings[2].forward_right()
-    total_c1(3)
-    b2_rings[1].forward_left()
-    b2_rings[1].forward_right()
     total_b1(3)
+    total_b2(1)
     pl.loop(7, 8)(rotated_chunk)
+    total_b2(0)
+    total_2(ring_c2, fc, ring_c3)
     total_b2(2)
-    total_b2(0)
-    total_b2(1)
-    total_2(ring_c2, fc, ring_c3)
     total_a1(1, 1)
     total_2(ring_a2, fa, ring_a3)
     total_b2(3)

time: 74.7 us -> 74.5 us (level)
  no operation moved by 1% of the time
where the time goes in v4:
time: 74.5 us; the launch traced here: 74 us
  Pallas kernels  73.3 us (98%)
    pallas_call x1, Pallas kernels, local(): pl.pallas_call(kernel, out_shape=shapes, in_specs=[any_spec] * 3, out_spe...  70.7 us
    pallas_call x1, Pallas kernels, local(): pl.pallas_call(hand_on, out_shape=shapes, in_specs=[any_spec] * 3, out_sp...  2.59 us

profile of v4, /device:TPU:1, one launch (start us, length us, event | category | flops | bytes accessed | tf_op | source)
XLA Modules:
  0.0 74.0 jit_solution(411603376300026270)
XLA Ops:
  0.6 70.7 %shard_map.58 = (f32[256,128]{1,0:T(8,128)}, f32[256,128]{1,0:T(8,128)}, f32[256,2048]{1,0:T(8,128)}) custom-call(f32[256,2048]{1,0:T(8,128)} %psi_hbm.1, f32[256,2048]{1,0:T(8,128)} %ham_hbm.1, f32[2048,2048]{1,0:T(8,128)} %rot_hbm.1), custom_call_target="tpu_custom_call" | custom-call | flops 19327352832 | bytes 25165824 | tf_op jit(solution)/shard_map/pallas_call | solution.py:589
  71.4 2.6 %shard_map.59 = (f32[256,128]{1,0:T(8,128)}, f32[256,128]{1,0:T(8,128)}, f32[256,2048]{1,0:T(8,128)}) custom-call(f32[256,128]{1,0:T(8,128)} %get-tuple-element.6.over_in, f32[256,128]{1,0:T(8,128)} %get-tuple-element.7.proj_in, f32[256,2048]{1,0:T(8,128)} %get-tuple-element.8.rotated_in), custom_call_target="tpu_custom_call" | custom-call | tf_op jit(solution)/shard_map/pallas_call | solution.py:615
